TPU v7x, 256 devices: a whole 4x4x8 slice. The times are simulated.
256 devices in a mesh: dp: 4 (over x), ep: 64 (over y, z, core).
Axes of the slice: x: 4, y: 4, z: 8, core: 2. Of those that a mesh axis runs over, the one named last changes fastest.
Arguments:
- tokens: bfloat16 [32768, 2048], P(('dp', 'ep'))
- cotangent: bfloat16 [32768, 2048], P(('dp', 'ep'))
- expert_ids: int32 [32768, 8], P(('dp', 'ep')), may hold values from 0 to 63, all different within a row; in each aligned block of 128 rows (0 to 127, 128 to 255, ...) at most 18 rows name the same one
- route_weights: bfloat16 [32768, 8], P(('dp', 'ep')), may hold values from 0.029907227 to 0.3984375
- weights: bfloat16 [64, 3, 2048, 384], P('ep')
- first_moment: bfloat16 [64, 3, 2048, 384], P('ep', None, 'dp'), may hold values from -4 to 4
- second_moment: bfloat16 [64, 3, 2048, 384], P('ep', None, 'dp'), may hold values from 0.049804688 to 0.5
Outputs:
- token_grad: bfloat16 [32768, 2048], P(('dp', 'ep'))
- routing_grad: bfloat16 [32768, 8], P(('dp', 'ep'))
- new_first: bfloat16 [64, 3, 2048, 384], P('ep', None, 'dp')
- new_second: bfloat16 [64, 3, 2048, 384], P('ep', None, 'dp')
- update: bfloat16 [64, 3, 2048, 384], P('ep', None, 'dp')
Inputs may be any that keep to these rules, and one draw needn't show every extreme that they name: `expert_ids`: among the 128 rows of one device no expert is named by more than 18 rows.
All inputs are finite; a program needn't handle non-finite values.
Results may differ from a plain program's by a relative error of at most 0.0057.
Values may be sent and summed in bfloat16 or wider, within the bound.
No kernel may reach another device: no remote copies, remote signals or barrier semaphores. Data moves between devices by JAX's collectives and lax.ppermute only.
A program may use at most 128 MiB of HBM per device.

v0:
```python
import jax
import jax.numpy as jnp
from jax import lax
from jax.experimental.layout import Layout, with_layout_constraint
from jax.sharding import Mesh, PartitionSpec as P

ADAM_STEP = 10
CORES = 2
BF16 = jnp.bfloat16
F32 = jnp.float32
INFO = 128


def plane(mesh):
    dp, ep = mesh.devices.shape
    y = 4
    z = ep // (y * CORES)
    return Mesh(mesh.devices.reshape(dp, y, z, CORES), ("x", "y", "z", "c"))


def on_device(tokens, cotangent, expert_ids, route_weights, weights, first_moment, second_moment):
    tok_count, model_width = tokens.shape
    topk_count = expert_ids.shape[1]
    hidden_units = weights.shape[3]
    ny, nz, nc = (lax.axis_size("y"), lax.axis_size("z"), lax.axis_size("c"))
    experts = ny * nz * nc
    capacity = (tok_count * topk_count * 9 + 8 * experts - 1) // (8 * experts)
    dests = ny * nc
    slots = nz * capacity
    yi, zi, ci = (lax.axis_index("y"), lax.axis_index("z"), lax.axis_index("c"))
    me = ((yi * nz + zi) * nc + ci).astype(F32)
    info = jnp.concatenate([expert_ids.astype(BF16), route_weights], 1)
    info = jnp.pad(info, ((0, 0), (0, INFO - 2 * topk_count)))
    info = with_layout_constraint(info, Layout((0, 1)))
    rows = with_layout_constraint(jnp.concatenate([tokens, info], 1), Layout((0, 1)))
    all_x = lax.all_gather(rows, "z", axis=0, tiled=True)
    all_cot = lax.all_gather(cotangent, "z", axis=0, tiled=True)
    ids = all_x[:, model_width : model_width + topk_count].astype(F32)
    dest = jnp.arange(dests, dtype=jnp.int32)
    dest_expert = ((dest // nc * nz + zi) * nc + dest % nc).astype(F32)
    match = jnp.any(ids[:, :, None] == dest_expert[None, None, :], 1)
    tri = jnp.tril(jnp.ones((tok_count, tok_count), BF16))
    count = jnp.einsum(
        "ab,sbd->sad",
        tri,
        match.astype(BF16).reshape(nz, tok_count, dests),
        preferred_element_type=F32,
    )
    base = (jnp.arange(nz, dtype=jnp.int32) * capacity - 1).astype(F32)[:, None, None]
    slot = jnp.where(match, (count + base).reshape(nz * tok_count, dests), -1.0)
    slot = lax.optimization_barrier(slot.T)
    picks = (
        slot[:, None, :] == jnp.arange(slots, dtype=jnp.int32).astype(F32)[None, :, None]
    ).astype(BF16)
    picks = lax.optimization_barrier(picks.reshape(dests * slots, nz * tok_count))

    def exchange(rows):
        width = rows.shape[1]
        out = lax.all_to_all(
            rows.reshape(dests, slots, width), ("y", "c"), split_axis=0, concat_axis=0, tiled=True
        )
        return out.reshape(dests * slots, width)

    recv = exchange(jnp.dot(picks, all_x, preferred_element_type=F32).astype(BF16))
    recv_cot = exchange(jnp.dot(picks, all_cot, preferred_element_type=F32).astype(BF16))
    recv_x = recv[:, :model_width]
    recv_ids = recv[:, model_width : model_width + topk_count].astype(F32)
    recv_rw = recv[:, model_width + topk_count : model_width + 2 * topk_count].astype(F32)
    mine = recv_ids == me
    row_weight = jnp.sum(jnp.where(mine, recv_rw, 0.0), 1, keepdims=True)
    w_gate, w_up, w_down = (weights[0, 0], weights[0, 1], weights[0, 2])
    gate_val = jnp.dot(recv_x, w_gate, preferred_element_type=F32)
    up_val = jnp.dot(recv_x, w_up, preferred_element_type=F32)
    sigmoid_gate = jax.nn.sigmoid(gate_val)
    activated = gate_val * sigmoid_gate
    hidden = lax.optimization_barrier((activated * up_val).astype(BF16))
    back_val = jnp.dot(recv_cot, w_down, preferred_element_type=F32)
    route_part = jnp.sum(hidden.astype(F32) * back_val, 1, keepdims=True).astype(BF16)
    scaled = row_weight * back_val
    dgate = (scaled * up_val * sigmoid_gate * (1.0 + gate_val * (1.0 - sigmoid_gate))).astype(BF16)
    dup = (scaled * activated).astype(BF16)
    down_cot = (row_weight * recv_cot.astype(F32)).astype(BF16)
    slot_back = jnp.einsum("rh,dh->rd", dgate, w_gate, preferred_element_type=F32)
    slot_back = slot_back + jnp.einsum("rh,dh->rd", dup, w_up, preferred_element_type=F32)
    route_rows = jnp.where(mine, route_part, jnp.zeros((), BF16))
    route_rows = jnp.pad(route_rows, ((0, 0), (0, INFO - topk_count)))
    send_back = jnp.concatenate([slot_back.astype(BF16), route_rows], 1)
    send_back, grad_x, grad_cot = lax.optimization_barrier((send_back, recv_x, down_cot))
    back_rows = exchange(send_back)
    partial = lax.dot_general(
        picks, back_rows, (((0,), (0,)), ((), ())), preferred_element_type=F32
    )
    total = lax.psum_scatter(partial.astype(BF16), "z", scatter_dimension=0, tiled=True)
    token_grad = total[:, :model_width]
    routing_grad = total[:, model_width : model_width + topk_count]
    grad_local = jnp.stack(
        [
            jnp.einsum("rd,rh->dh", grad_x, dgate, preferred_element_type=F32).astype(BF16),
            jnp.einsum("rd,rh->dh", grad_x, dup, preferred_element_type=F32).astype(BF16),
            jnp.einsum("rd,rh->dh", grad_cot, hidden, preferred_element_type=F32).astype(BF16),
        ],
        0,
    )
    grad_share = lax.psum_scatter(grad_local, "x", scatter_dimension=1, tiled=True).astype(F32)[
        None
    ]
    square = jnp.sum(grad_share * grad_share)
    square = jnp.broadcast_to(square, (experts, 1, 128))
    square = lax.all_to_all(square, ("y", "z", "c"), split_axis=0, concat_axis=0, tiled=True)
    square_sum = lax.psum(jnp.sum(square[:, 0, 0]), "x")
    param_count = 3.0 * experts * model_width * hidden_units
    root_mean = jnp.sqrt(square_sum / param_count + 1e-06)
    clip_factor = jnp.minimum(1.0, 0.5 / root_mean)
    clipped = clip_factor * grad_share
    first_next = 0.9 * first_moment.astype(F32) + 0.1 * clipped
    second_next = 0.95 * second_moment.astype(F32) + 0.05 * clipped * clipped
    update = (
        first_next
        / (1.0 - 0.9**ADAM_STEP)
        / (jnp.sqrt(second_next / (1.0 - 0.95**ADAM_STEP)) + 1e-08)
    )
    return (
        token_grad,
        routing_grad,
        first_next.astype(BF16),
        second_next.astype(BF16),
        update.astype(BF16),
    )


def solution(mesh):
    tok = P(("x", "y", "z", "c"), None)
    ep = ("y", "z", "c")
    state = P(ep, None, "x", None)
    return jax.shard_map(
        on_device,
        mesh=plane(mesh),
        in_specs=(tok, tok, tok, tok, P(ep, None, None, None), state, state),
        out_specs=(tok, tok, state, state, state),
        check_vma=False,
    )
```

profile of v0, /device:TPU:1, one launch (start us, length us, event | category | flops | bytes accessed | tf_op | source)
XLA Modules:
  0.0 375.6 jit_solution(4099123066367515721)
XLA Ops:
  7.2 0.0 all-gather.3.cloned.1.call-start
  7.2 0.7 convert_element_type.110
  7.9 0.7 pad_maximum_fusion.1
  8.6 0.1 copy.53
  8.7 1.9 fusion.34
  10.6 0.0 all-gather.3.cloned.1.call-update
  10.6 0.0 all-gather.5.cloned.1.call-start
  10.7 0.7 all-gather.5.cloned.1.call-update
  11.4 0.1 eq.47
  11.5 60.1 %all-gather.3.cloned.1.call-done = bf16[1024,2176]{1,0:T(8,128)(2,1)} async-done(((bf16[128,2176]{1,0:T(8,128)(2,1)}), bf16[1024,2176]{1,0:T(8,128)(2,1)}) %all-gather.3.cloned.1.call-update) | async-done | bytes 4456464 | tf_op jit(solution)/shard_map/all_gather | solution.py:36
  71.6 1.0 slice_convert_fusion
  72.6 0.2 copy.54
  72.8 0.1 compare_reduce_fusion
  72.9 0.1 fusion.33
  73.0 0.5 fusion.3
  73.5 9.6 %convolution_convert_fusion = bf16[1152,2176]{1,0:T(8,128)(2,1)} fusion(bf16[1152,1024]{1,0:T(8,128)(2,1)S(1)} %fusion.3, bf16[1024,2176]{1,0:T(8,128)(2,1)} %all-gather.3.cloned.1.call-done), kind=kOutput, calls=%fused_computation | convolution fusion | flops 5136334848 | bytes 11829248 | tf_op jit(solution)/shard_map/dot_general | solution.py:64
  83.1 5.3 %all-to-all-start = ((bf16[8,144,2176]{2,1,0:T(8,128)(2,1)}), bf16[8,144,2176]{2,1,0:T(8,128)(2,1)}, u32[]{:S(2)}, u32[]{:S(2)}) async-start(bf16[8,144,2176]{2,1,0:T(8,128)(2,1)} %bitcast.80), calls=%async_computation | async-start | bytes 10027008 | tf_op jit(solution)/shard_map/all_to_all | solution.py:59
  88.5 38.3 %all-gather.5.cloned.1.call-done = bf16[1024,2048]{1,0:T(8,128)(2,1)} async-done(((bf16[128,2048]{1,0:T(8,128)(2,1)}), bf16[1024,2048]{1,0:T(8,128)(2,1)}) %all-gather.5.cloned.1.call-update) | async-done | bytes 4194320 | tf_op jit(solution)/shard_map/all_gather | solution.py:37
  126.8 8.8 %convolution_convert_fusion.1 = bf16[1152,2048]{1,0:T(8,128)(2,1)} fusion(bf16[1152,1024]{1,0:T(8,128)(2,1)S(1)} %fusion.3, bf16[1024,2048]{1,0:T(8,128)(2,1)} %all-gather.5.cloned.1.call-done), kind=kOutput, calls=%fused_computation.6 | convolution fusion | flops 4834197504 | bytes 11272192 | tf_op jit(solution)/shard_map/dot_general | solution.py:65
  135.6 10.4 %all-to-all-done = bf16[8,144,2176]{2,1,0:T(8,128)(2,1)} async-done(((bf16[8,144,2176]{2,1,0:T(8,128)(2,1)}), bf16[8,144,2176]{2,1,0:T(8,128)(2,1)}, u32[]{:S(2)}, u32[]{:S(2)}) %all-to-all-start) | async-done | bytes 5013536 | tf_op jit(solution)/shard_map/all_to_all | solution.py:59
  146.0 5.4 %all-to-all-start.1 = ((bf16[8,144,2048]{2,1,0:T(8,128)(2,1)}), bf16[8,144,2048]{2,1,0:T(8,128)(2,1)}, u32[]{:S(2)}, u32[]{:S(2)}) async-start(bf16[8,144,2048]{2,1,0:T(8,128)(2,1)} %bitcast.82), calls=%async_computation.1 | async-start | bytes 9437184 | tf_op jit(solution)/shard_map/all_to_all | solution.py:59
  151.5 0.0 reduce-scatter.5.cloned.1.call-start
  151.5 5.3 %slice.43 = bf16[1152,2048]{1,0:T(8,128)(2,1)} slice(bf16[1152,2176]{1,0:T(8,128)(2,1)} %bitcast.7), slice={[0:1152], [0:2048]} | slice | bytes 9437184 | tf_op jit(solution)/shard_map/slice | solution.py:66
  156.8 1.4 select_reduce_fusion
  158.1 6.4 %fusion.19 = f32[1152,384]{0,1:T(8,128)} fusion(bf16[1,3,2048,384]{3,2,1,0:T(8,128)(2,1)} %param.11, bf16[1152,2176]{1,0:T(8,128)(2,1)} %bitcast.7), kind=kOutput, calls=%fused_computation.39 | convolution fusion | flops 1811939328 | bytes 8060928 | tf_op jit(solution)/shard_map/dot_general | solution.py:73
  164.5 6.3 %fusion.16 = f32[1152,384]{0,1:T(8,128)} fusion(bf16[1,3,2048,384]{3,2,1,0:T(8,128)(2,1)} %param.11, bf16[1152,2176]{1,0:T(8,128)(2,1)} %bitcast.7), kind=kOutput, calls=%fused_computation.36 | convolution fusion | flops 1811939328 | bytes 8060928 | tf_op jit(solution)/shard_map/dot_general | solution.py:72
  170.8 35.1 %all-to-all-done.1 = bf16[8,144,2048]{2,1,0:T(8,128)(2,1)} async-done(((bf16[8,144,2048]{2,1,0:T(8,128)(2,1)}), bf16[8,144,2048]{2,1,0:T(8,128)(2,1)}, u32[]{:S(2)}, u32[]{:S(2)}) %all-to-all-start.1) | async-done | bytes 4718624 | tf_op jit(solution)/shard_map/all_to_all | solution.py:59
  205.9 7.9 %multiply_convert_fusion.2 = (bf16[1152,384]{0,1:T(8,128)(2,1)}, bf16[1152,384]{0,1:T(8,128)(2,1)S(1)}, bf16[1152,384]{0,1:T(8,128)(2,1)S(1)}, f32[1152,384]{0,1:T(8,128)S(1)}) fusion(f32[1152]{0:T(1024)S(1)} %select_reduce_fusion, f32[1152,384]{0,1:T(8,128)} %fusion.16, f32[1152,384]{0,1:T(8,128)} %fusion.19, bf16[1152,2048]{1,0:T(8,128)(2,1)} %bitcast.9, ...), kind=kOutput, calls=%fused_computation.30 | convolution fusion | flops 1819017216 | bytes 14258688 | tf_op jit(solution)/shard_map/dot_general | solution.py:77
  213.8 0.2 multiply_reduce_fusion
  214.0 1.2 broadcast_select_fusion
  215.3 0.0 slice-done.2
  215.3 0.0 slice-done.3
  215.3 2.7 fusion.14
  218.0 0.0 copy-done.2
  218.0 0.0 slice-start
  218.0 4.5 %fusion.1 = bf16[1152,2048]{1,0:T(8,128)(2,1)S(1)} fusion(f32[1152,2048]{1,0:T(8,128)S(1)} %fusion.14, bf16[1152,384]{0,1:T(8,128)(2,1)} %get-tuple-element.41, bf16[1,3,2048,384]{3,2,1,0:T(8,128)(2,1)S(1)} %bitcast.86), kind=kOutput, calls=%fused_computation.5 | convolution fusion | flops 1816657920 | bytes 16613376 | tf_op jit(solution)/shard_map/rh,dh->rd/dot_general | solution.py:84
  222.5 0.0 slice-start.1
  222.5 2.7 fusion.2
  225.2 3.2 multiply_convert_fusion
  228.4 0.0 slice-done
  228.5 0.0 slice-done.1
  228.5 0.0 copy-done.4
  228.5 2.8 fusion.6
  231.3 0.0 copy-start.3
  231.3 2.8 fusion.5
  234.2 0.0 copy-done.3
  234.2 2.8 fusion.7
  237.0 2.5 pad_maximum_fusion
  239.5 0.0 reduce-scatter.5.cloned.1.call-update
  239.5 0.0 reduce-scatter.3.cloned.1.call-start
  239.6 62.5 %all_to_all.20 = bf16[8,144,2176]{2,1,0:T(8,128)(2,1)S(1)} all-to-all(bf16[8,144,2176]{2,1,0:T(8,128)(2,1)} %bitcast.79), channel_id=1, replica_groups=mesh['x'=4,'y'=4,'z'=8,'c'=2] {'y','c'}, dimensions={0} | all-to-all | bytes 10027008 | tf_op jit(solution)/shard_map/all_to_all | solution.py:59
  302.1 7.9 %convolution_convert_fusion.2 = bf16[1024,2176]{1,0:T(8,128)(2,1)} fusion(bf16[1152,1024]{1,0:T(8,128)(2,1)S(1)} %fusion.3, bf16[1152,2176]{1,0:T(8,128)(2,1)S(1)} %bitcast.81), kind=kOutput, calls=%fused_computation.7 | convolution fusion | flops 5136056320 | bytes 11829248 | tf_op jit(solution)/shard_map/dot_general | solution.py:90
  310.0 0.0 reduce-scatter.3.cloned.1.call-update
  310.0 0.0 reduce-scatter.5.cloned.1.call-done
  310.0 2.6 fusion.10
  312.7 0.7 broadcast_in_dim.44
  313.3 15.9 %all_to_all.21 = f32[64,1,128]{2,1,0:T(1,128)S(1)} all-to-all(f32[64,1,128]{2,1,0:T(1,128)S(1)} %broadcast_in_dim.44), channel_id=1, replica_groups=mesh['x'=4,'y'=4,'z'=8,'c'=2] {'y','z','c'}, dimensions={0} | all-to-all | bytes 65536 | tf_op jit(solution)/shard_map/all_to_all | solution.py:109
  329.2 0.7 slice_reduce_fusion
  329.9 9.8 %psum.7 = f32[]{:T(128)} all-reduce(f32[]{:T(128)} %slice_reduce_fusion), channel_id=1, replica_groups=mesh['x'=4,'y'=4,'z'=8,'c'=2] {'x'}, use_global_device_ids=true, to_apply=%region_7.8 | all-reduce | flops 1 | bytes 8 | tf_op jit(solution)/shard_map/psum | solution.py:110
  340.4 4.8 %divide_convert_fusion = (bf16[1,3,512,384]{3,2,1,0:T(8,128)(2,1)}, bf16[1,3,512,384]{3,2,1,0:T(8,128)(2,1)}, bf16[1,3,512,384]{3,2,1,0:T(8,128)(2,1)}) fusion(bf16[3,512,384]{2,1,0:T(8,128)(2,1)} %reduce-scatter.5.cloned.1.call-done, bf16[1,3,512,384]{3,2,1,0:T(8,128)(2,1)S(1)} %copy-done, bf16[1,3,512,384]{3,2,1,0:T(8,128)(2,1)S(1)} %copy-done.1, f32[]{:T(128)S(6)} %min.3), kind=kLoop, calls=%fused_computation.27 | loop fusion | flops 10616832 | bytes 7077892 | tf_op jit(solution)/shard_map/convert_element_type | solution.py:127
  345.3 20.6 %reduce-scatter.3.cloned.1.call-done = bf16[128,2176]{1,0:T(8,128)(2,1)} async-done(((bf16[1024,2176]{1,0:T(8,128)(2,1)}), bf16[128,2176]{1,0:T(8,128)(2,1)}) %reduce-scatter.3.cloned.1.call-update) | async-done | bytes 557072 | tf_op jit(solution)/shard_map/reduce_scatter | solution.py:93
  365.8 0.8 slice.45
  366.6 0.7 copy.61
  367.2 1.9 slice.44
  (14 shorter events, 0.0 us)
Async XLA Ops:
  7.2 64.5 %all-gather.3.cloned.1.call-start = ((), (), s32[]{:S(2)}) async-start(), calls=%async_computation.6 | async-start | bytes 5013504 | tf_op jit(solution)/shard_map/all_gather | solution.py:36
  10.6 116.2 %all-gather.5.cloned.1.call-start = ((), (), s32[]{:S(2)}) async-start(), calls=%async_computation.7 | async-start | bytes 4718592 | tf_op jit(solution)/shard_map/all_gather | solution.py:37
  83.1 62.9 %all-to-all-start = ((bf16[8,144,2176]{2,1,0:T(8,128)(2,1)}), bf16[8,144,2176]{2,1,0:T(8,128)(2,1)}, u32[]{:S(2)}, u32[]{:S(2)}) async-start(bf16[8,144,2176]{2,1,0:T(8,128)(2,1)} %bitcast.80), calls=%async_computation | async-start | bytes 10027008 | tf_op jit(solution)/shard_map/all_to_all | solution.py:59
  146.0 59.9 %all-to-all-start.1 = ((bf16[8,144,2048]{2,1,0:T(8,128)(2,1)}), bf16[8,144,2048]{2,1,0:T(8,128)(2,1)}, u32[]{:S(2)}, u32[]{:S(2)}) async-start(bf16[8,144,2048]{2,1,0:T(8,128)(2,1)} %bitcast.82), calls=%async_computation.1 | async-start | bytes 9437184 | tf_op jit(solution)/shard_map/all_to_all | solution.py:59
  151.5 158.5 %reduce-scatter.5.cloned.1.call-start = ((), (), s32[]{:S(2)}) async-start(), calls=%async_computation.9 | async-start | bytes 5898240 | tf_op jit(solution)/shard_map/reduce_scatter | solution.py:104
  205.9 9.4 %slice-start.2 = ((s8[4718592]{0:T(1024)(128)(4,1)}), s8[4194304]{0:T(1024)(128)(4,1)S(1)}, s32[]{:S(2)}) async-start(s8[4718592]{0:T(1024)(128)(4,1)} %bitcast.85), calls=%async_computation.12 | async-start | bytes 8388608
  205.9 9.4 %slice-start.3 = ((s8[4718592]{0:T(1024)(128)(4,1)}), s8[524288]{0:T(1024)(128)(4,1)S(1)}, s32[]{:S(2)}) async-start(s8[4718592]{0:T(1024)(128)(4,1)} %bitcast.85), calls=%async_computation.13 | async-start | bytes 1048576
  213.8 4.2 %copy-start.2 = (bf16[1152,384]{0,1:T(8,128)(2,1)}, bf16[1152,384]{0,1:T(8,128)(2,1)S(1)}, u32[]{:S(2)}) copy-start(bf16[1152,384]{0,1:T(8,128)(2,1)S(1)} %get-tuple-element.43) | copy-start | bytes 2654212
  218.0 10.5 %slice-start = ((s8[4718592]{0:T(1024)(128)(4,1)}), s8[4194304]{0:T(1024)(128)(4,1)S(1)}, s32[]{:S(2)}) async-start(s8[4718592]{0:T(1024)(128)(4,1)} %bitcast.83), calls=%async_computation.10 | async-start | bytes 8388608
  222.5 6.0 %slice-start.1 = ((s8[4718592]{0:T(1024)(128)(4,1)}), s8[524288]{0:T(1024)(128)(4,1)S(1)}, s32[]{:S(2)}) async-start(s8[4718592]{0:T(1024)(128)(4,1)} %bitcast.83), calls=%async_computation.11 | async-start | bytes 1048576
  225.2 3.3 copy-start.4
  231.3 2.8 copy-start.3
  239.5 126.3 %reduce-scatter.3.cloned.1.call-start = ((), (), s32[]{:S(2)}) async-start(), calls=%async_computation.8 | async-start | bytes 5013504 | tf_op jit(solution)/shard_map/reduce_scatter | solution.py:93
  310.0 30.5 %copy-start = (bf16[1,3,512,384]{3,2,1,0:T(8,128)(2,1)S(1)}, bf16[1,3,512,384]{3,2,1,0:T(8,128)(2,1)}, u32[]{:S(2)}) copy-start(bf16[1,3,512,384]{3,2,1,0:T(8,128)(2,1)} %param.13) | copy-start | bytes 3538948
  310.0 30.5 %copy-start.1 = (bf16[1,3,512,384]{3,2,1,0:T(8,128)(2,1)S(1)}, bf16[1,3,512,384]{3,2,1,0:T(8,128)(2,1)}, u32[]{:S(2)}) copy-start(bf16[1,3,512,384]{3,2,1,0:T(8,128)(2,1)} %param.12) | copy-start | bytes 3538948
Sparse Core Ops, SparseCore 0:
  10.7 60.8 all-gather.2
  73.4 53.3 all-gather.4
  239.6 50.6 reduce-scatter.4
  310.1 55.6 reduce-scatter.2
where the time goes:
time: 376 us
  waiting for transfers between devices  165 us (44%)
  blocking collectives  88.2 us (23%)
  matrix products  62.5 us (17%)
  other arithmetic  24.3 us (6%)
  between operations  14.7 us (4%)
  starting transfers between devices  10.9 us (3%)
  local copies, waits for them, and re-layouts  9.63 us (3%)
    all_to_all x1, blocking collectives, exchange(): lax.all_to_all(rows.reshape(dests, slots, width), ('y', 'c'), split_axis=...  62.5 us
    all_gather x1, waiting for transfers between devices, on_device(): all_x = lax.all_gather(rows, 'z', axis=0, tiled=True)  60.1 us
    all_to_all x2, waiting for transfers between devices, exchange(): lax.all_to_all(rows.reshape(dests, slots, width), ('y', 'c'), split_axis=...  45.6 us
    all_gather x1, waiting for transfers between devices, on_device(): all_cot = lax.all_gather(cotangent, 'z', axis=0, tiled=True)  38.3 us
    reduce_scatter x1, waiting for transfers between devices, on_device(): lax.psum_scatter(partial.astype(BF16), 'z', scatter_dimension=0, tiled=True)  20.6 us
    all_to_all x1, blocking collectives, on_device(): lax.all_to_all(square, ('y', 'z', 'c'), split_axis=0, concat_axis=0, tile...  15.9 us
    all_to_all x2, starting transfers between devices, exchange(): lax.all_to_all(rows.reshape(dests, slots, width), ('y', 'c'), split_axis=...  10.8 us
    psum x1, blocking collectives, on_device(): square_sum = lax.psum(jnp.sum(square[:, 0, 0]), 'x')  9.81 us
  transfers between devices with their start and end apart: 6, of which 5 were waited for; matrix products, arithmetic and copies ran while one was open for 15% of the time, Pallas kernels for 0%

commit v1 on v0

--- a/solution.py
+++ b/solution.py
@@ -33,7 +33,8 @@
     info = jnp.pad(info, ((0, 0), (0, INFO - 2 * topk_count)))
     info = with_layout_constraint(info, Layout((0, 1)))
     rows = with_layout_constraint(jnp.concatenate([tokens, info], 1), Layout((0, 1)))
-    all_x = lax.all_gather(rows, "z", axis=0, tiled=True)
+    stack = jnp.stack([rows] * lax.axis_size("z"))
+    all_x = jnp.concatenate(lax.all_to_all(stack, "z", 0, 0), axis=0)
     all_cot = lax.all_gather(cotangent, "z", axis=0, tiled=True)
     ids = all_x[:, model_width : model_width + topk_count].astype(F32)
     dest = jnp.arange(dests, dtype=jnp.int32)

time: 376 us -> 478 us (1.27); the launches traced: 376 us -> 472 us
  waiting for transfers between devices: 165 us -> 246 us
  local copies, waits for them, and re-layouts: 9.63 us -> 20 us
  starting transfers between devices: 10.9 us -> 20 us
    all_to_all x0 -> x1, waiting for transfers between devices: none -> 141 us  [on_device(): all_x = jnp.concatenate(lax.all_to_all(stack, 'z', 0, 0), axis=0)]
    all_gather x1 -> x0, waiting for transfers between devices: 60.1 us -> none  [on_device(): all_x = lax.all_gather(rows, 'z', axis=0, tiled=True)]
    all_gather x1, waiting for transfers between devices: 38.3 us -> 0.01 us  [on_device(): all_cot = lax.all_gather(cotangent, 'z', axis=0, tiled=True)]
    all_to_all x2, waiting for transfers between devices: 45.6 us -> 83.4 us  [exchange(): lax.all_to_all(rows.reshape(dests, slots, width), ('y', 'c'), split_axis=...]
    all_to_all x0 -> x1, starting transfers between devices: none -> 9 us  [on_device(): all_x = jnp.concatenate(lax.all_to_all(stack, 'z', 0, 0), axis=0)]
    all_to_all x0 -> x1, local copies, waits for them, and re-layouts: none -> 6.45 us  [on_device(): all_x = jnp.concatenate(lax.all_to_all(stack, 'z', 0, 0), axis=0)]
  transfers between devices with their start and end apart: 6 -> 6, of which waited for: 5 -> 4; matrix products, arithmetic and copies ran while one was open for 15% -> 13% of each run, Pallas kernels for 0% -> 0%
where the time goes in v1:
time: 478 us; the launch traced here: 472 us
  waiting for transfers between devices  246 us (51%)
  blocking collectives  86.1 us (18%)
  matrix products  62.5 us (13%)
  other arithmetic  22.5 us (5%)
  local copies, waits for them, and re-layouts  20 us (4%)
  starting transfers between devices  20 us (4%)
  between operations  14.9 us (3%)
    all_to_all x1, waiting for transfers between devices, on_device(): all_x = jnp.concatenate(lax.all_to_all(stack, 'z', 0, 0), axis=0)  141 us
    all_to_all x2, waiting for transfers between devices, exchange(): lax.all_to_all(rows.reshape(dests, slots, width), ('y', 'c'), split_axis=...  83.4 us
    all_to_all x1, blocking collectives, exchange(): lax.all_to_all(rows.reshape(dests, slots, width), ('y', 'c'), split_axis=...  62.7 us
    reduce_scatter x1, waiting for transfers between devices, on_device(): lax.psum_scatter(partial.astype(BF16), 'z', scatter_dimension=0, tiled=True)  20.5 us
    all_to_all x1, blocking collectives, on_device(): lax.all_to_all(square, ('y', 'z', 'c'), split_axis=0, concat_axis=0, tile...  13.5 us
    all_to_all x2, starting transfers between devices, exchange(): lax.all_to_all(rows.reshape(dests, slots, width), ('y', 'c'), split_axis=...  10.4 us
    psum x1, blocking collectives, on_device(): square_sum = lax.psum(jnp.sum(square[:, 0, 0]), 'x')  9.89 us
    dot_general x1, matrix products, on_device(): jnp.dot(picks, all_x, preferred_element_type=F32).astype(BF16)  9.65 us
  transfers between devices with their start and end apart: 6, of which 4 were waited for; matrix products, arithmetic and copies ran while one was open for 13% of the time, Pallas kernels for 0%

profile of v1, /device:TPU:1, one launch (start us, length us, event | category | flops | bytes accessed | tf_op | source)
XLA Modules:
  0.0 471.6 jit_solution(952504690946329932)
XLA Ops:
  7.2 0.7 convert_element_type.110
  7.9 0.7 pad_maximum_fusion.1
  8.5 0.1 copy.64
  8.7 1.1 fusion.34
  9.8 0.3 copy.65
  10.1 2.7 stack.10
  12.8 9.0 %all-to-all-start = ((bf16[8,128,2176]{1,2,0:T(8,128)(2,1)}), bf16[8,128,2176]{1,2,0:T(8,128)(2,1)}, u32[]{:S(2)}, u32[]{:S(2)}) async-start(bf16[8,128,2176]{1,2,0:T(8,128)(2,1)} %stack.10), calls=%async_computation | async-start | bytes 8912896 | tf_op jit(solution)/shard_map/all_to_all | solution.py:37
  21.8 0.0 all-gather.2.cloned.1.call-start
  21.8 0.7 all-gather.2.cloned.1.call-update
  22.5 0.1 eq.47
  22.7 140.8 %all-to-all-done = bf16[8,128,2176]{1,2,0:T(8,128)(2,1)} async-done(((bf16[8,128,2176]{1,2,0:T(8,128)(2,1)}), bf16[8,128,2176]{1,2,0:T(8,128)(2,1)}, u32[]{:S(2)}, u32[]{:S(2)}) %all-to-all-start) | async-done | bytes 4456480 | tf_op jit(solution)/shard_map/all_to_all | solution.py:37
  163.5 6.5 %copy.66 = bf16[8,128,2176]{2,1,0:T(8,128)(2,1)} copy(bf16[8,128,2176]{1,2,0:T(8,128)(2,1)} %all-to-all-done) | data formatting | bytes 8912896 | tf_op jit(solution)/shard_map/all_to_all | solution.py:37
  169.9 1.0 slice.40
  170.9 0.1 copy.78
  171.0 0.1 compare_reduce_fusion
  171.1 0.1 fusion.33
  171.2 0.5 fusion.3
  171.7 9.7 %convolution_convert_fusion = bf16[1152,2176]{1,0:T(8,128)(2,1)} fusion(bf16[1152,1024]{1,0:T(8,128)(2,1)S(1)} %fusion.3, bf16[1024,2176]{1,0:T(8,128)(2,1)} %bitcast.84), kind=kOutput, calls=%fused_computation | convolution fusion | flops 5136334848 | bytes 11829248 | tf_op jit(solution)/shard_map/dot_general | solution.py:65
  181.4 5.0 %all-to-all-start.1 = ((bf16[8,144,2176]{2,1,0:T(8,128)(2,1)}), bf16[8,144,2176]{2,1,0:T(8,128)(2,1)}, u32[]{:S(2)}, u32[]{:S(2)}) async-start(bf16[8,144,2176]{2,1,0:T(8,128)(2,1)} %bitcast.81), calls=%async_computation.1 | async-start | bytes 10027008 | tf_op jit(solution)/shard_map/all_to_all | solution.py:60
  186.4 8.8 %convolution_convert_fusion.1 = bf16[1152,2048]{1,0:T(8,128)(2,1)} fusion(bf16[1152,1024]{1,0:T(8,128)(2,1)S(1)} %fusion.3, bf16[1024,2048]{1,0:T(8,128)(2,1)} %all-gather.2.cloned.1.call-done), kind=kOutput, calls=%fused_computation.6 | convolution fusion | flops 4834197504 | bytes 11272192 | tf_op jit(solution)/shard_map/dot_general | solution.py:66
  195.2 48.8 %all-to-all-done.1 = bf16[8,144,2176]{2,1,0:T(8,128)(2,1)} async-done(((bf16[8,144,2176]{2,1,0:T(8,128)(2,1)}), bf16[8,144,2176]{2,1,0:T(8,128)(2,1)}, u32[]{:S(2)}, u32[]{:S(2)}) %all-to-all-start.1) | async-done | bytes 5013536 | tf_op jit(solution)/shard_map/all_to_all | solution.py:60
  244.0 5.4 %all-to-all-start.2 = ((bf16[8,144,2048]{2,1,0:T(8,128)(2,1)}), bf16[8,144,2048]{2,1,0:T(8,128)(2,1)}, u32[]{:S(2)}, u32[]{:S(2)}) async-start(bf16[8,144,2048]{2,1,0:T(8,128)(2,1)} %bitcast.85), calls=%async_computation.2 | async-start | bytes 9437184 | tf_op jit(solution)/shard_map/all_to_all | solution.py:60
  249.4 0.5 reduce-scatter.5.cloned.1.call-start
  249.9 5.3 %slice.43 = bf16[1152,2048]{1,0:T(8,128)(2,1)} slice(bf16[1152,2176]{1,0:T(8,128)(2,1)} %bitcast.8), slice={[0:1152], [0:2048]} | slice | bytes 9437184 | tf_op jit(solution)/shard_map/slice | solution.py:67
  255.2 1.3 select_reduce_fusion
  256.5 6.3 %fusion.19 = f32[1152,384]{0,1:T(8,128)} fusion(bf16[1,3,2048,384]{3,2,1,0:T(8,128)(2,1)} %param.11, bf16[1152,2176]{1,0:T(8,128)(2,1)} %bitcast.8), kind=kOutput, calls=%fused_computation.39 | convolution fusion | flops 1811939328 | bytes 8060928 | tf_op jit(solution)/shard_map/dot_general | solution.py:74
  262.9 6.3 %fusion.16 = f32[1152,384]{0,1:T(8,128)} fusion(bf16[1,3,2048,384]{3,2,1,0:T(8,128)(2,1)} %param.11, bf16[1152,2176]{1,0:T(8,128)(2,1)} %bitcast.8), kind=kOutput, calls=%fused_computation.36 | convolution fusion | flops 1811939328 | bytes 8060928 | tf_op jit(solution)/shard_map/dot_general | solution.py:73
  269.2 34.7 %all-to-all-done.2 = bf16[8,144,2048]{2,1,0:T(8,128)(2,1)} async-done(((bf16[8,144,2048]{2,1,0:T(8,128)(2,1)}), bf16[8,144,2048]{2,1,0:T(8,128)(2,1)}, u32[]{:S(2)}, u32[]{:S(2)}) %all-to-all-start.2) | async-done | bytes 4718624 | tf_op jit(solution)/shard_map/all_to_all | solution.py:60
  303.8 7.9 %multiply_convert_fusion.2 = (bf16[1152,384]{0,1:T(8,128)(2,1)}, bf16[1152,384]{0,1:T(8,128)(2,1)S(1)}, bf16[1152,384]{0,1:T(8,128)(2,1)S(1)}, f32[1152,384]{0,1:T(8,128)S(1)}) fusion(f32[1152]{0:T(1024)S(1)} %select_reduce_fusion, f32[1152,384]{0,1:T(8,128)} %fusion.16, f32[1152,384]{0,1:T(8,128)} %fusion.19, bf16[1152,2048]{1,0:T(8,128)(2,1)} %bitcast.10, ...), kind=kOutput, calls=%fused_computation.30 | convolution fusion | flops 1819017216 | bytes 14258688 | tf_op jit(solution)/shard_map/dot_general | solution.py:78
  311.7 0.2 multiply_reduce_fusion
  312.0 1.2 broadcast_select_fusion
  313.2 0.0 slice-done.2
  313.2 0.0 slice-done.3
  313.2 2.7 fusion.14
  315.9 0.0 copy-done.2
  315.9 0.0 slice-start
  315.9 4.4 fusion.1
  320.4 0.0 slice-start.1
  320.4 2.7 fusion.2
  323.1 3.2 multiply_convert_fusion
  326.3 0.0 slice-done
  326.3 0.0 slice-done.1
  326.3 0.0 copy-done.4
  326.4 2.8 fusion.6
  329.2 0.0 copy-start.3
  329.2 2.8 fusion.5
  332.0 2.8 fusion.7
  334.9 2.5 pad_maximum_fusion
  337.4 0.0 reduce-scatter.5.cloned.1.call-update
  337.4 0.0 reduce-scatter.3.cloned.1.call-start
  337.4 62.7 %all_to_all.25 = bf16[8,144,2176]{2,1,0:T(8,128)(2,1)S(1)} all-to-all(bf16[8,144,2176]{2,1,0:T(8,128)(2,1)} %bitcast.80), channel_id=1, replica_groups=mesh['x'=4,'y'=4,'z'=8,'c'=2] {'y','c'}, dimensions={0} | all-to-all | bytes 10027008 | tf_op jit(solution)/shard_map/all_to_all | solution.py:60
  400.1 7.9 %convolution_convert_fusion.2 = bf16[1024,2176]{1,0:T(8,128)(2,1)} fusion(bf16[1152,1024]{1,0:T(8,128)(2,1)S(1)} %fusion.3, bf16[1152,2176]{1,0:T(8,128)(2,1)S(1)} %bitcast.82), kind=kOutput, calls=%fused_computation.7 | convolution fusion | flops 5136056320 | bytes 11829248 | tf_op jit(solution)/shard_map/dot_general | solution.py:91
  408.0 0.0 reduce-scatter.3.cloned.1.call-update
  408.1 0.0 reduce-scatter.5.cloned.1.call-done
  408.1 2.6 fusion.10
  410.7 0.7 broadcast_in_dim.44
  411.4 13.5 %all_to_all.26 = f32[64,1,128]{2,1,0:T(1,128)S(1)} all-to-all(f32[64,1,128]{2,1,0:T(1,128)S(1)} %broadcast_in_dim.44), channel_id=1, replica_groups=mesh['x'=4,'y'=4,'z'=8,'c'=2] {'y','z','c'}, dimensions={0} | all-to-all | bytes 65536 | tf_op jit(solution)/shard_map/all_to_all | solution.py:110
  424.9 0.7 slice_reduce_fusion
  425.6 9.9 %psum.7 = f32[]{:T(128)} all-reduce(f32[]{:T(128)} %slice_reduce_fusion), channel_id=1, replica_groups=mesh['x'=4,'y'=4,'z'=8,'c'=2] {'x'}, use_global_device_ids=true, to_apply=%region_7.8 | all-reduce | flops 1 | bytes 8 | tf_op jit(solution)/shard_map/psum | solution.py:111
  436.2 4.8 %divide_convert_fusion = (bf16[1,3,512,384]{3,2,1,0:T(8,128)(2,1)}, bf16[1,3,512,384]{3,2,1,0:T(8,128)(2,1)}, bf16[1,3,512,384]{3,2,1,0:T(8,128)(2,1)}) fusion(bf16[3,512,384]{2,1,0:T(8,128)(2,1)} %reduce-scatter.5.cloned.1.call-done, bf16[1,3,512,384]{3,2,1,0:T(8,128)(2,1)S(1)} %copy-done, bf16[1,3,512,384]{3,2,1,0:T(8,128)(2,1)S(1)} %copy-done.1, f32[]{:T(128)S(6)} %min.3), kind=kLoop, calls=%fused_computation.27 | loop fusion | flops 10616832 | bytes 7077892 | tf_op jit(solution)/shard_map/convert_element_type | solution.py:128
  441.0 20.5 %reduce-scatter.3.cloned.1.call-done = bf16[128,2176]{1,0:T(8,128)(2,1)} async-done(((bf16[1024,2176]{1,0:T(8,128)(2,1)}), bf16[128,2176]{1,0:T(8,128)(2,1)}) %reduce-scatter.3.cloned.1.call-update) | async-done | bytes 557072 | tf_op jit(solution)/shard_map/reduce_scatter | solution.py:94
  461.6 0.8 slice.45
  462.3 0.7 copy.74
  463.0 1.9 slice.44
  (17 shorter events, 0.0 us)
Async XLA Ops:
  12.8 150.7 %all-to-all-start = ((bf16[8,128,2176]{1,2,0:T(8,128)(2,1)}), bf16[8,128,2176]{1,2,0:T(8,128)(2,1)}, u32[]{:S(2)}, u32[]{:S(2)}) async-start(bf16[8,128,2176]{1,2,0:T(8,128)(2,1)} %stack.10), calls=%async_computation | async-start | bytes 8912896 | tf_op jit(solution)/shard_map/all_to_all | solution.py:37
  21.8 164.6 %all-gather.2.cloned.1.call-start = ((), (), s32[]{:S(2)}) async-start(), calls=%async_computation.7 | async-start | bytes 4718592 | tf_op jit(solution)/shard_map/all_gather | solution.py:38
  181.4 62.6 %all-to-all-start.1 = ((bf16[8,144,2176]{2,1,0:T(8,128)(2,1)}), bf16[8,144,2176]{2,1,0:T(8,128)(2,1)}, u32[]{:S(2)}, u32[]{:S(2)}) async-start(bf16[8,144,2176]{2,1,0:T(8,128)(2,1)} %bitcast.81), calls=%async_computation.1 | async-start | bytes 10027008 | tf_op jit(solution)/shard_map/all_to_all | solution.py:60
  244.0 59.9 %all-to-all-start.2 = ((bf16[8,144,2048]{2,1,0:T(8,128)(2,1)}), bf16[8,144,2048]{2,1,0:T(8,128)(2,1)}, u32[]{:S(2)}, u32[]{:S(2)}) async-start(bf16[8,144,2048]{2,1,0:T(8,128)(2,1)} %bitcast.85), calls=%async_computation.2 | async-start | bytes 9437184 | tf_op jit(solution)/shard_map/all_to_all | solution.py:60
  249.4 158.7 %reduce-scatter.5.cloned.1.call-start = ((), (), s32[]{:S(2)}) async-start(), calls=%async_computation.9 | async-start | bytes 5898240 | tf_op jit(solution)/shard_map/reduce_scatter | solution.py:105
  303.8 9.4 %slice-start.2 = ((s8[4718592]{0:T(1024)(128)(4,1)}), s8[4194304]{0:T(1024)(128)(4,1)S(1)}, s32[]{:S(2)}) async-start(s8[4718592]{0:T(1024)(128)(4,1)} %bitcast.88), calls=%async_computation.12 | async-start | bytes 8388608
  303.8 9.4 %slice-start.3 = ((s8[4718592]{0:T(1024)(128)(4,1)}), s8[524288]{0:T(1024)(128)(4,1)S(1)}, s32[]{:S(2)}) async-start(s8[4718592]{0:T(1024)(128)(4,1)} %bitcast.88), calls=%async_computation.13 | async-start | bytes 1048576
  311.7 4.2 copy-start.2
  315.9 10.4 %slice-start = ((s8[4718592]{0:T(1024)(128)(4,1)}), s8[4194304]{0:T(1024)(128)(4,1)S(1)}, s32[]{:S(2)}) async-start(s8[4718592]{0:T(1024)(128)(4,1)} %bitcast.86), calls=%async_computation.10 | async-start | bytes 8388608
  320.4 6.0 %slice-start.1 = ((s8[4718592]{0:T(1024)(128)(4,1)}), s8[524288]{0:T(1024)(128)(4,1)S(1)}, s32[]{:S(2)}) async-start(s8[4718592]{0:T(1024)(128)(4,1)} %bitcast.86), calls=%async_computation.11 | async-start | bytes 1048576
  323.1 3.3 copy-start.4
  329.2 2.8 copy-start.3
  337.4 124.2 %reduce-scatter.3.cloned.1.call-start = ((), (), s32[]{:S(2)}) async-start(), calls=%async_computation.8 | async-start | bytes 5013504 | tf_op jit(solution)/shard_map/reduce_scatter | solution.py:94
  408.0 28.2 %copy-start = (bf16[1,3,512,384]{3,2,1,0:T(8,128)(2,1)S(1)}, bf16[1,3,512,384]{3,2,1,0:T(8,128)(2,1)}, u32[]{:S(2)}) copy-start(bf16[1,3,512,384]{3,2,1,0:T(8,128)(2,1)} %param.13) | copy-start | bytes 3538948
  408.0 28.2 %copy-start.1 = (bf16[1,3,512,384]{3,2,1,0:T(8,128)(2,1)S(1)}, bf16[1,3,512,384]{3,2,1,0:T(8,128)(2,1)}, u32[]{:S(2)}) copy-start(bf16[1,3,512,384]{3,2,1,0:T(8,128)(2,1)} %param.12) | copy-start | bytes 3538948
Sparse Core Ops, SparseCore 0:
  24.4 135.5 all-gather.1
  337.5 48.1 reduce-scatter.4
  408.2 53.3 reduce-scatter.2
